TPU v7x, 512 devices: a whole 4x4x16 slice. The times are simulated.
512 devices in a mesh: member: 16 (over x, z_hi), slab: 32 (over y, z_lo, core).
Axes of the slice: x: 4, y: 4, z: 16 (z_hi: 4, z_lo: 4; z = z_hi * 4 + z_lo), core: 2. Of those that a mesh axis runs over, the one named last changes fastest.
Arguments:
- fluid_head_start: float32 [192, 512, 128], P('member', 'slab'), may hold values from -6 to 6
- conductivity_matrix: float32 [192, 512, 128], P('member', 'slab'), may hold values from 0.1 to 1
- well_rates: float32 [512, 128], P('slab'), may hold values from -3 to 3
- cell_layer: int32 [512, 128], P('slab'), may hold values from 0 to 7
- pixel_coords: int32 [2, 4096], replicated, may hold values from 0 to 63
- obs_index: int32 [1024], replicated, may hold values from 0 to 4095
- obs_value: float32 [1024], replicated, may hold values from -0.6 to 0.6
- obs_sigma: float32 [1024], replicated, may hold values from 0.05 to 0.5
Outputs:
- analysed: float32 [192, 512, 128], P('member', 'slab')
- subsidence: float32 [4096, 192], P(('member', 'slab'))
All inputs are finite; a program needn't handle non-finite values.
Results may differ from a plain program's by a relative error of at most 0.00028.
Values sent between devices are 32-bit elements; how exact they have to be, the bound alone decides.
A program may use at most 64 MiB of HBM per device.

v0:
```python
import math
import jax
import jax.numpy as jnp
from jax import lax
from jax.sharding import PartitionSpec as P

STEPS = 4
time_step = 0.15
pixel_span = 64.0
top_depth = 2.0


def padded(value, sides, width):
    for axis, dim in sides:
        size, length = (lax.axis_size(axis), value.shape[dim])
        up = [(i, (i + 1) % size) for i in range(size - 1)]
        down = [(j, i) for i, j in up]
        last = lax.slice_in_dim(value, length - width, length, axis=dim)
        initial = lax.slice_in_dim(value, 0, width, axis=dim)
        before = lax.ppermute(last, axis, up)
        after = lax.ppermute(initial, axis, down)
        value = jnp.concatenate([before, value, after], axis=dim)
    return value


def advance_in_time(fluid_head_grid, perm_field, source, open_faces):
    mobility = perm_field * (1.0 + 0.5 * jnp.tanh(fluid_head_grid))
    sample_vectors, height, across_cells = fluid_head_grid.shape
    across = 0.5 * (mobility[:, 1:] + mobility[:, :-1]) * open_faces[None, :, None]
    flux_rows = across * (fluid_head_grid[:, 1:] - fluid_head_grid[:, :-1])
    zero_row = jnp.zeros((sample_vectors, 1, across_cells), fluid_head_grid.dtype)
    inflow = jnp.concatenate([flux_rows, zero_row], 1) - jnp.concatenate([zero_row, flux_rows], 1)
    along = 0.5 * (mobility[:, :, 1:] + mobility[:, :, :-1])
    flux_cols = along * (fluid_head_grid[:, :, 1:] - fluid_head_grid[:, :, :-1])
    zero_col = jnp.zeros((sample_vectors, height, 1), fluid_head_grid.dtype)
    inflow = inflow + (
        jnp.concatenate([flux_cols, zero_col], 2) - jnp.concatenate([zero_col, flux_cols], 2)
    )
    return fluid_head_grid + time_step * (inflow + source[None])


def kernel_rows(pixel_x, pixel_y, cell_x, cell_y, depth, volume):
    delta_x = cell_x[None, :] - pixel_x[:, None]
    delta_y = cell_y[None, :] - pixel_y[:, None]
    radius = delta_x * delta_x + delta_y * delta_y + depth[None, :] * depth[None, :]
    return volume * depth[None, :] / (radius * jnp.sqrt(radius))


def gram_terms(predicted, obs_value, obs_sigma, owned):
    centre = jnp.mean(predicted, axis=1)
    anomaly = predicted - centre[:, None]
    inverse_var = 1.0 / (obs_sigma * obs_sigma)
    weighted = anomaly * inverse_var[:, None]
    gram = lax.dot_general(
        anomaly, weighted, (((0,), (0,)), ((), ())), precision=lax.Precision.HIGHEST
    )
    rhs = jnp.dot(owned * (obs_value - centre), weighted, precision=lax.Precision.HIGHEST)
    return (gram, rhs)


def finish(gram, rhs, sample_vector_pile):
    sample_vectors = sample_vector_pile.shape[0]
    ident = jnp.eye(sample_vectors, dtype=gram.dtype)
    gram = gram + (sample_vectors - 1.0) * ident
    factor = jnp.linalg.cholesky(gram)
    inverse = jax.scipy.linalg.solve_triangular(factor, ident, lower=True)
    weights = jnp.dot(
        inverse.T,
        jnp.dot(inverse, rhs, precision=lax.Precision.HIGHEST),
        precision=lax.Precision.HIGHEST,
    )
    transform = jnp.sqrt(sample_vectors - 1.0) * inverse.T
    mix = weights[:, None] + transform
    centre = jnp.mean(sample_vector_pile, axis=0)
    spread = sample_vector_pile - centre[None]
    return centre[None] + lax.dot_general(
        mix, spread, (((0,), (0,)), ((), ())), precision=lax.Precision.HIGHEST
    )


def face_mask(first_global, height, total_rows):
    index = first_global + jnp.arange(height - 1, dtype=jnp.int32)
    return ((index >= 0) & (index + 1 <= total_rows - 1)).astype(jnp.float32)


def shards(
    fluid_head_start,
    conductivity_matrix,
    well_rates,
    cell_layer,
    pixel_coords,
    obs_index,
    obs_value,
    obs_sigma,
):
    local_members, slab_rows, across_cells = fluid_head_start.shape
    member_count = lax.axis_size("member")
    slab_count = lax.axis_size("slab")
    slab_index = lax.axis_index("slab")
    member_index = lax.axis_index("member")
    total_rows = slab_rows * slab_count
    rim_width = STEPS
    static = jnp.concatenate([conductivity_matrix, well_rates[None]], 0)
    static_ext = padded(static, (("slab", 1),), rim_width)
    permeability_extended = static_ext[:-1]
    source_extended = static_ext[-1]
    fluid_head_grid = padded(fluid_head_start, (("slab", 1),), STEPS)
    open_faces = face_mask(slab_index * slab_rows - STEPS, slab_rows + 2 * STEPS, total_rows)
    for repeat in range(STEPS):
        fluid_head_grid = advance_in_time(
            fluid_head_grid, permeability_extended, source_extended, open_faces
        )
    predicted_ensemble = fluid_head_grid[:, STEPS : STEPS + slab_rows]
    collected_states = lax.all_to_all(
        predicted_ensemble, "member", split_axis=1, concat_axis=0, tiled=True
    )
    sample_vectors = collected_states.shape[0]
    sub_rows = collected_states.shape[1]
    sample_vector_pile = collected_states.reshape(sample_vectors, sub_rows * across_cells)
    row_global = (
        slab_index * slab_rows + member_index * sub_rows + jnp.arange(sub_rows, dtype=jnp.int32)
    )
    row_pos = (row_global.astype(jnp.float32) + 0.5) * (pixel_span / total_rows)
    col_pos = (jnp.arange(across_cells).astype(jnp.float32) + 0.5) * (pixel_span / across_cells)
    cell_x = jnp.broadcast_to(row_pos[:, None], (sub_rows, across_cells)).reshape(-1)
    cell_y = col_pos[None, :].reshape(-1)
    layers = lax.dynamic_slice_in_dim(cell_layer, member_index * sub_rows, sub_rows, 0).astype(
        jnp.float32
    )
    depth = (top_depth + layers).reshape(-1)
    volume = pixel_span * pixel_span / (total_rows * across_cells)
    pixel_f = pixel_coords.astype(jnp.float32)
    pixel_total = pixel_coords.shape[1]
    own_rows = pixel_total // (member_count * slab_count)
    own_first = lax.axis_index(("member", "slab")) * own_rows
    block = math.gcd(pixel_total, 512)

    def pixel_block(offset):
        coords = lax.dynamic_slice_in_dim(pixel_f, offset, block, 1)
        kern = kernel_rows(coords[0], coords[1], cell_x, cell_y, depth, volume)
        return lax.dot_general(
            kern, sample_vector_pile, (((1,), (1,)), ((), ())), precision=lax.Precision.HIGHEST
        )

    offsets = 0 + block * jnp.arange(pixel_total // block, dtype=jnp.int32)
    whole = lax.psum(
        lax.map(pixel_block, offsets).reshape(pixel_total, sample_vectors), ("member", "slab")
    )
    own_part = lax.dynamic_slice_in_dim(whole, own_first, own_rows, 0)
    predicted = jnp.take(whole, obs_index, axis=0)
    gram, rhs = gram_terms(predicted, obs_value, obs_sigma, jnp.ones_like(obs_value))
    analysed = finish(gram, rhs, sample_vector_pile).reshape(sample_vectors, sub_rows, across_cells)
    returned = lax.all_to_all(analysed, "member", split_axis=0, concat_axis=1, tiled=True)
    return (returned, own_part)


def solution(mesh):
    return jax.shard_map(
        shards,
        mesh=mesh,
        in_specs=(
            P("member", "slab", None),
            P("member", "slab", None),
            P("slab", None),
            P("slab", None),
            P(),
            P(),
            P(),
            P(),
        ),
        out_specs=(P("member", "slab", None), P(("member", "slab"), None)),
        check_vma=False,
    )
```

profile of v0, /device:TPU:8, one launch (start us, length us, event | category | flops | bytes accessed | tf_op | source)
XLA Modules:
  0.0 677.4 jit_solution(5419804613752783939)
XLA Ops:
  7.2 0.8 fusion.83
  8.0 1.9 collective-permute-start
  10.0 6.3 collective-permute-start.1
  16.3 0.9 copy.28
  17.2 0.7 pad_maximum_fusion.7
  17.9 1.9 collective-permute-start.2
  19.9 6.3 collective-permute-start.3
  26.3 0.9 copy_dynamic-update-slice_fusion
  27.2 0.6 collective-permute-done.3
  27.8 0.7 pad_maximum_fusion.8
  28.5 0.7 pad_maximum_fusion
  29.3 0.2 fusion.40
  29.6 0.1 add_multiply_fusion.3
  29.8 0.2 fusion.38
  30.0 0.1 add_multiply_fusion.2
  30.3 0.2 fusion.36
  30.4 0.1 add_multiply_fusion.1
  30.7 0.2 fusion.34
  30.9 0.8 slice_add_fusion.8
  31.6 17.7 %all-to-all-start = ((f32[12,16,128]{2,0,1:T(8,128)}), f32[12,16,128]{2,0,1:T(8,128)S(1)}, u32[]{:S(2)}, u32[]{:S(2)}) async-start(f32[12,16,128]{2,0,1:T(8,128)} %slice_add_fusion.8), calls=%async_computation | async-start | bytes 262144 | tf_op jit(solution)/shard_map/all_to_all | solution.py:114
  49.4 0.7 fusion.81
  50.1 15.0 %all-to-all-done = f32[12,16,128]{2,0,1:T(8,128)S(1)} async-done(((f32[12,16,128]{2,0,1:T(8,128)}), f32[12,16,128]{2,0,1:T(8,128)S(1)}, u32[]{:S(2)}, u32[]{:S(2)}) %all-to-all-start) | async-done | bytes 98336 | tf_op jit(solution)/shard_map/all_to_all | solution.py:114
  65.1 24.8 %while.14 = (s32[]{:T(128)}, f32[8,512,192]{1,2,0:T(8,128)S(1)}, f32[1,128]{1,0:T(1,128)S(1)}, f32[1,1]{1,0:T(1,128)}, s32[8]{0:T(128)S(1)}, /*index=5*/f32[2,40...) while((s32[]{:T(128)}, f32[8,512,192]{1,2,0:T(8,128)S(1)}, ...), condition=%wide.region_2.3_spmd.clone, body=%wide.region_1.2_spmd.clone.sunk | while | flops 151389696 | bytes 507079 | solution.py:147
  65.1 0.6 dynamic_slice.27
  67.5 0.7 fusion.99
  68.2 0.6 dynamic_slice.27
  70.6 0.7 fusion.99
  71.3 0.6 dynamic_slice.27
  73.7 0.7 fusion.99
  74.4 0.6 dynamic_slice.27
  76.8 0.7 fusion.99
  77.5 0.6 dynamic_slice.27
  79.9 0.7 fusion.99
  80.6 0.6 dynamic_slice.27
  83.0 0.7 fusion.99
  83.7 0.6 dynamic_slice.27
  86.1 0.7 fusion.99
  86.8 0.6 dynamic_slice.27
  89.2 0.7 fusion.99
  89.9 3.4 copy.29
  93.4 0.6 copy-done.1
  94.1 486.0 %all-reduce.21.cloned.1.call-done = f32[4096,192]{1,0:T(8,128)} async-done(((f32[4096,192]{1,0:T(8,128)}), f32[4096,192]{1,0:T(8,128)}) %all-reduce.21.cloned.1.call-update) | async-done | bytes 3145744 | tf_op jit(solution)/shard_map/psum | solution.py:146
  580.1 5.8 gather_fusion
  585.9 0.4 select_reduce_fusion
  586.3 2.5 fusion.17
  589.0 11.7 %cholesky.50 = f32[128,128]{1,0:T(8,128)S(1)} custom-call(f32[128,128]{1,0:T(8,128)S(1)} %cholesky.121), custom_call_target="Cholesky" | custom-call | tf_op jit(solution)/shard_map/jit(cholesky)/cholesky | solution.py:65
  600.8 0.9 fusion.19
  601.6 0.6 compare_reduce_fusion.1
  602.3 9.8 %custom-call.15 = f32[1,128,128]{1,2,0:T(8,128)S(1)} custom-call(f32[1,128,128]{2,1,0:T(8,128)S(1)} %get-tuple-element.153), custom_call_target="InvertDiagBlocksLowerTriangular" | custom-call | tf_op jit(solution)/shard_map/jit(cholesky)/cholesky | solution.py:65
  612.1 0.2 constant_dynamic-update-slice_fusion.3
  612.3 0.2 convolution_subtract_fusion.1
  612.5 5.8 cholesky.108
  618.3 0.6 compare_reduce_fusion
  620.4 19.9 %custom-call.16 = f32[2,128,128]{1,2,0:T(8,128)S(1)} custom-call(f32[2,128,128]{2,1,0:T(8,128)S(1)} %pad_maximum_fusion.2), custom_call_target="InvertDiagBlocksLowerTriangular" | custom-call | tf_op jit(solution)/shard_map/jit(_solve_triangular)/triangular_solve | solution.py:66
  640.3 0.3 fusion.59
  640.6 0.3 convolution_subtract_fusion
  640.9 0.3 fusion.69
  641.3 0.2 convolution_bitcast_fusion.1
  641.5 0.2 fusion.42
  641.7 1.4 convolution_add_fusion
  643.1 11.5 %all-to-all-start.1 = ((f32[192,1,128]{2,1,0:T(1,128)}), f32[192,1,128]{2,1,0:T(1,128)S(1)}, u32[]{:S(2)}, u32[]{:S(2)}) async-start(f32[192,1,128]{2,1,0:T(1,128)} %bitcast.21), calls=%async_computation.1 | async-start | bytes 196608 | tf_op jit(solution)/shard_map/all_to_all | solution.py:153
  654.7 1.3 constant_dynamic-slice_fusion
  656.0 13.9 %all-to-all-done.1 = f32[192,1,128]{2,1,0:T(1,128)S(1)} async-done(((f32[192,1,128]{2,1,0:T(1,128)}), f32[192,1,128]{2,1,0:T(1,128)S(1)}, u32[]{:S(2)}, u32[]{:S(2)}) %all-to-all-start.1) | async-done | bytes 98336 | tf_op jit(solution)/shard_map/all_to_all | solution.py:153
  669.9 0.6 copy.39
  (70 shorter events, 1.8 us)
Async XLA Ops:
  8.0 18.2 %collective-permute-start = (f32[12,4,128]{2,0,1:T(8,128)S(1)}, f32[12,4,128]{2,0,1:T(8,128)S(1)}, u32[]{:S(2)}, u32[]{:S(2)}) collective-permute-start(f32[12,4,128]{2,0,1:T(8,128)S(1)} %copy.37), channel_id=1, source_target_pairs={{0,1},{1,2},{2,3},{3,4},{4,5},{5,6},{6,7},{7,8},{8,9},{9,10},{10,1... | collective-permute-start | bytes 73736 | tf_op jit(solution)/shard_map/ppermute | solution.py:20
  10.0 17.2 %collective-permute-start.1 = (f32[12,4,128]{2,0,1:T(8,128)S(1)}, f32[12,4,128]{2,0,1:T(8,128)S(1)}, u32[]{:S(2)}, u32[]{:S(2)}) collective-permute-start(f32[12,4,128]{2,0,1:T(8,128)S(1)} %copy.38), channel_id=1, source_target_pairs={{1,0},{2,1},{3,2},{4,3},{5,4},{6,5},{7,6},{8,7},{9,8},{10,9},{11,1... | collective-permute-start | bytes 73736 | tf_op jit(solution)/shard_map/ppermute | solution.py:21
  17.9 9.3 %collective-permute-start.2 = (f32[13,4,128]{2,0,1:T(8,128)S(1)}, f32[13,4,128]{2,0,1:T(8,128)S(1)}, u32[]{:S(2)}, u32[]{:S(2)}) collective-permute-start(f32[13,4,128]{2,0,1:T(8,128)S(1)} %get-tuple-element.148), channel_id=1, source_target_pairs={{0,1},{1,2},{2,3},{3,4},{4,5},{5,6},{6,7},{7,8},{8,9},{9,10},{10,1... | collective-permute-start | bytes 79880 | tf_op jit(solution)/shard_map/ppermute | solution.py:20
  19.9 7.9 %collective-permute-start.3 = (f32[13,4,128]{2,0,1:T(8,128)S(1)}, f32[13,4,128]{2,0,1:T(8,128)S(1)}, u32[]{:S(2)}, u32[]{:S(2)}) collective-permute-start(f32[13,4,128]{2,0,1:T(8,128)S(1)} %get-tuple-element.149), channel_id=1, source_target_pairs={{1,0},{2,1},{3,2},{4,3},{5,4},{6,5},{7,6},{8,7},{9,8},{10,9},{11,1... | collective-permute-start | bytes 79880 | tf_op jit(solution)/shard_map/ppermute | solution.py:21
  30.2 19.2 %copy-start = (s32[2,4096]{1,0:T(2,128)S(1)}, s32[2,4096]{1,0:T(2,128)}, u32[]{:S(2)}) copy-start(s32[2,4096]{1,0:T(2,128)} %param.14) | copy-start | bytes 98308
  31.6 33.5 %all-to-all-start = ((f32[12,16,128]{2,0,1:T(8,128)}), f32[12,16,128]{2,0,1:T(8,128)S(1)}, u32[]{:S(2)}, u32[]{:S(2)}) async-start(f32[12,16,128]{2,0,1:T(8,128)} %slice_add_fusion.8), calls=%async_computation | async-start | bytes 262144 | tf_op jit(solution)/shard_map/all_to_all | solution.py:114
  49.3 530.8 %all-reduce.21.cloned.1.call-start = ((), (), s32[]{:S(2)}) async-start(), calls=%async_computation.2 | async-start | bytes 8388608 | tf_op jit(solution)/shard_map/psum | solution.py:146
  93.3 0.7 copy-start.1
  93.3 0.7 copy-start.2
  94.1 492.2 %copy-start.3 = (f32[1024]{0:T(1024)S(1)}, f32[1024]{0:T(1024)}, u32[]{:S(2)}) copy-start(f32[1024]{0:T(1024)} %param.16) | copy-start | bytes 12292
  643.1 26.8 %all-to-all-start.1 = ((f32[192,1,128]{2,1,0:T(1,128)}), f32[192,1,128]{2,1,0:T(1,128)S(1)}, u32[]{:S(2)}, u32[]{:S(2)}) async-start(f32[192,1,128]{2,1,0:T(1,128)} %bitcast.21), calls=%async_computation.1 | async-start | bytes 196608 | tf_op jit(solution)/shard_map/all_to_all | solution.py:153
Sparse Core Ops, SparseCore 0:
  93.5 486.5 all-reduce.20
where the time goes:
time: 678 us; the launch traced here: 677 us
  waiting for transfers between devices  515 us (76%)
  other arithmetic  55.2 us (8%)
  starting transfers between devices  45.8 us (7%)
  local copies, waits for them, and re-layouts  19.3 us (3%)
  between operations  15.8 us (2%)
  loops' own time  13.8 us (2%)
  matrix products  12.1 us (2%)
    psum x1, waiting for transfers between devices, shards(): lax.psum(lax.map(pixel_block, offsets).reshape(pixel_total, sample_vector...  486 us
    another operation x7, other arithmetic, finish(): factor = jnp.linalg.cholesky(gram)  28.7 us
    another operation x6, other arithmetic, finish(): inverse = jax.scipy.linalg.solve_triangular(factor, ident, lower=True)  20 us
    all_to_all x1, starting transfers between devices, shards(): lax.all_to_all(predicted_ensemble, 'member', split_axis=1, concat_axis=0,...  17.7 us
    all_to_all x1, waiting for transfers between devices, shards(): lax.all_to_all(predicted_ensemble, 'member', split_axis=1, concat_axis=0,...  15 us
    all_to_all x1, waiting for transfers between devices, shards(): lax.all_to_all(analysed, 'member', split_axis=0, concat_axis=1, tiled=True)  13.9 us
    another operation x1, loops' own time, shards(): lax.map(pixel_block, offsets).reshape(pixel_total, sample_vectors)  13.8 us
  transfers between devices with their start and end apart: 7, of which 4 were waited for; matrix products, arithmetic and copies ran while one was open for 1% of the time, Pallas kernels for 0%

commit v1 on v0

--- a/solution.py
+++ b/solution.py
@@ -143,9 +143,9 @@
         )
 
     offsets = 0 + block * jnp.arange(pixel_total // block, dtype=jnp.int32)
-    whole = lax.psum(
-        lax.map(pixel_block, offsets).reshape(pixel_total, sample_vectors), ("member", "slab")
-    )
+    whole = lax.map(pixel_block, offsets).reshape(pixel_total, sample_vectors)
+    for name in ("member", "slab"):
+        whole = lax.psum(whole, name)
     own_part = lax.dynamic_slice_in_dim(whole, own_first, own_rows, 0)
     predicted = jnp.take(whole, obs_index, axis=0)
     gram, rhs = gram_terms(predicted, obs_value, obs_sigma, jnp.ones_like(obs_value))

time: 678 us -> 889 us (1.31)
  the two profiles are of different devices: /device:TPU:8 before, /device:TPU:2 now
where the time goes in v1:
time: 889 us; the launch traced here: 888 us
  waiting for transfers between devices  732 us (82%)
  other arithmetic  55.2 us (6%)
  starting transfers between devices  40.6 us (5%)
  local copies, waits for them, and re-layouts  18.5 us (2%)
  between operations  15.8 us (2%)
  loops' own time  13.8 us (2%)
  matrix products  12.1 us (1%)
    psum x2, waiting for transfers between devices, shards(): whole = lax.psum(whole, name)  703 us
    another operation x7, other arithmetic, finish(): factor = jnp.linalg.cholesky(gram)  28.7 us
    another operation x6, other arithmetic, finish(): inverse = jax.scipy.linalg.solve_triangular(factor, ident, lower=True)  20 us
  transfers between devices with their start and end apart: 8, of which 5 were waited for; matrix products, arithmetic and copies ran while one was open for 1% of the time, Pallas kernels for 0%

profile of v1, /device:TPU:2, one launch (start us, length us, event | category | flops | bytes accessed | tf_op | source)
XLA Modules:
  0.0 888.4 jit_solution(936272523450704151)
XLA Ops:
  7.2 0.8 fusion.83
  8.0 1.7 collective-permute-start
  9.8 1.3 collective-permute-start.1
  11.1 0.9 copy.28
  12.0 0.7 pad_maximum_fusion.7
  12.7 4.7 collective-permute-start.2
  17.5 1.3 collective-permute-start.3
  18.8 0.9 copy_dynamic-update-slice_fusion
  19.8 2.0 collective-permute-done.3
  21.8 0.7 pad_maximum_fusion.8
  22.5 0.7 pad_maximum_fusion
  23.3 0.2 fusion.40
  23.6 0.1 add_multiply_fusion.3
  23.8 0.2 fusion.38
  24.0 0.1 add_multiply_fusion.2
  24.3 0.2 fusion.36
  24.7 0.2 fusion.34
  24.9 0.8 slice_add_fusion.8
  25.6 17.2 %all-to-all-start = ((f32[12,16,128]{2,0,1:T(8,128)}), f32[12,16,128]{2,0,1:T(8,128)S(1)}, u32[]{:S(2)}, u32[]{:S(2)}) async-start(f32[12,16,128]{2,0,1:T(8,128)} %slice_add_fusion.8), calls=%async_computation | async-start | bytes 262144 | tf_op jit(solution)/shard_map/all_to_all | solution.py:114
  43.0 0.7 fusion.81
  43.7 15.5 %all-to-all-done = f32[12,16,128]{2,0,1:T(8,128)S(1)} async-done(((f32[12,16,128]{2,0,1:T(8,128)}), f32[12,16,128]{2,0,1:T(8,128)S(1)}, u32[]{:S(2)}, u32[]{:S(2)}) %all-to-all-start) | async-done | bytes 98336 | tf_op jit(solution)/shard_map/all_to_all | solution.py:114
  59.1 24.8 %while.14 = (s32[]{:T(128)}, f32[8,512,192]{1,2,0:T(8,128)S(1)}, f32[1,128]{1,0:T(1,128)S(1)}, f32[1,1]{1,0:T(1,128)}, s32[8]{0:T(128)S(1)}, /*index=5*/f32[2,40...) while((s32[]{:T(128)}, f32[8,512,192]{1,2,0:T(8,128)S(1)}, ...), condition=%wide.region_2.3_spmd.clone, body=%wide.region_1.2_spmd.clone.sunk | while | flops 151389696 | bytes 507079 | solution.py:146
  59.1 0.6 dynamic_slice.27
  61.5 0.7 fusion.99
  62.2 0.6 dynamic_slice.27
  64.6 0.7 fusion.99
  65.3 0.6 dynamic_slice.27
  67.7 0.7 fusion.99
  68.4 0.6 dynamic_slice.27
  70.8 0.7 fusion.99
  71.5 0.6 dynamic_slice.27
  73.9 0.7 fusion.99
  74.6 0.6 dynamic_slice.27
  77.0 0.7 fusion.99
  77.7 0.6 dynamic_slice.27
  80.1 0.7 fusion.99
  80.8 0.6 dynamic_slice.27
  83.2 0.7 fusion.99
  83.9 3.4 copy.29
  87.4 0.2 all-reduce.24.cloned.1.call-start
  87.6 398.7 %all-reduce.22.cloned.1.call-done = f32[4096,192]{1,0:T(8,128)} async-done(((f32[4096,192]{1,0:T(8,128)}), f32[4096,192]{1,0:T(8,128)}) %all-reduce.22.cloned.1.call-update) | async-done | bytes 3145744 | tf_op jit(solution)/shard_map/psum | solution.py:148
  486.5 303.9 %all-reduce.24.cloned.1.call-done = f32[4096,192]{1,0:T(8,128)} async-done(((f32[4096,192]{1,0:T(8,128)}), f32[4096,192]{1,0:T(8,128)}) %all-reduce.24.cloned.1.call-update) | async-done | bytes 3145744 | tf_op jit(solution)/shard_map/psum | solution.py:148
  790.5 5.6 gather_fusion
  796.1 0.4 select_reduce_fusion
  796.5 2.5 fusion.17
  799.2 11.7 %cholesky.50 = f32[128,128]{1,0:T(8,128)S(1)} custom-call(f32[128,128]{1,0:T(8,128)S(1)} %cholesky.121), custom_call_target="Cholesky" | custom-call | tf_op jit(solution)/shard_map/jit(cholesky)/cholesky | solution.py:65
  811.0 0.9 fusion.19
  811.9 0.6 compare_reduce_fusion.1
  812.5 9.8 %custom-call.15 = f32[1,128,128]{1,2,0:T(8,128)S(1)} custom-call(f32[1,128,128]{2,1,0:T(8,128)S(1)} %get-tuple-element.153), custom_call_target="InvertDiagBlocksLowerTriangular" | custom-call | tf_op jit(solution)/shard_map/jit(cholesky)/cholesky | solution.py:65
  822.3 0.2 constant_dynamic-update-slice_fusion.3
  822.5 0.2 convolution_subtract_fusion.1
  822.7 5.8 cholesky.108
  828.6 0.6 compare_reduce_fusion
  830.7 19.9 %custom-call.16 = f32[2,128,128]{1,2,0:T(8,128)S(1)} custom-call(f32[2,128,128]{2,1,0:T(8,128)S(1)} %pad_maximum_fusion.2), custom_call_target="InvertDiagBlocksLowerTriangular" | custom-call | tf_op jit(solution)/shard_map/jit(_solve_triangular)/triangular_solve | solution.py:66
  850.6 0.3 fusion.59
  850.9 0.3 convolution_subtract_fusion
  851.2 0.3 fusion.69
  851.5 0.2 convolution_bitcast_fusion.1
  851.7 0.2 fusion.42
  852.0 1.3 convolution_add_fusion
  853.3 14.1 %all-to-all-start.1 = ((f32[192,1,128]{2,1,0:T(1,128)}), f32[192,1,128]{2,1,0:T(1,128)S(1)}, u32[]{:S(2)}, u32[]{:S(2)}) async-start(f32[192,1,128]{2,1,0:T(1,128)} %bitcast.21), calls=%async_computation.1 | async-start | bytes 196608 | tf_op jit(solution)/shard_map/all_to_all | solution.py:153
  867.4 1.3 constant_dynamic-slice_fusion
  868.7 12.2 %all-to-all-done.1 = f32[192,1,128]{2,1,0:T(1,128)S(1)} async-done(((f32[192,1,128]{2,1,0:T(1,128)}), f32[192,1,128]{2,1,0:T(1,128)S(1)}, u32[]{:S(2)}, u32[]{:S(2)}) %all-to-all-start.1) | async-done | bytes 98336 | tf_op jit(solution)/shard_map/all_to_all | solution.py:153
  880.9 0.6 copy.39
  (73 shorter events, 1.9 us)
Async XLA Ops:
  8.0 10.8 %collective-permute-start = (f32[12,4,128]{2,0,1:T(8,128)S(1)}, f32[12,4,128]{2,0,1:T(8,128)S(1)}, u32[]{:S(2)}, u32[]{:S(2)}) collective-permute-start(f32[12,4,128]{2,0,1:T(8,128)S(1)} %copy.37), channel_id=1, source_target_pairs={{0,1},{1,2},{2,3},{3,4},{4,5},{5,6},{6,7},{7,8},{8,9},{9,10},{10,1... | collective-permute-start | bytes 73736 | tf_op jit(solution)/shard_map/ppermute | solution.py:20
  9.8 10.0 %collective-permute-start.1 = (f32[12,4,128]{2,0,1:T(8,128)S(1)}, f32[12,4,128]{2,0,1:T(8,128)S(1)}, u32[]{:S(2)}, u32[]{:S(2)}) collective-permute-start(f32[12,4,128]{2,0,1:T(8,128)S(1)} %copy.38), channel_id=1, source_target_pairs={{1,0},{2,1},{3,2},{4,3},{5,4},{6,5},{7,6},{8,7},{9,8},{10,9},{11,1... | collective-permute-start | bytes 73736 | tf_op jit(solution)/shard_map/ppermute | solution.py:21
  12.7 7.0 collective-permute-start.2
  17.5 4.3 collective-permute-start.3
  24.2 18.7 %copy-start = (s32[2,4096]{1,0:T(2,128)S(1)}, s32[2,4096]{1,0:T(2,128)}, u32[]{:S(2)}) copy-start(s32[2,4096]{1,0:T(2,128)} %param.14) | copy-start | bytes 98308
  25.6 33.5 %all-to-all-start = ((f32[12,16,128]{2,0,1:T(8,128)}), f32[12,16,128]{2,0,1:T(8,128)S(1)}, u32[]{:S(2)}, u32[]{:S(2)}) async-start(f32[12,16,128]{2,0,1:T(8,128)} %slice_add_fusion.8), calls=%async_computation | async-start | bytes 262144 | tf_op jit(solution)/shard_map/all_to_all | solution.py:114
  42.8 443.5 %all-reduce.22.cloned.1.call-start = ((), (), s32[]{:S(2)}) async-start(), calls=%async_computation.2 | async-start | bytes 8388608 | tf_op jit(solution)/shard_map/psum | solution.py:148
  87.3 399.1 %copy-start.1 = (s32[1024]{0:T(1024)S(1)}, s32[1024]{0:T(1024)}, u32[]{:S(2)}) copy-start(s32[1024]{0:T(1024)} %param.15) | copy-start | bytes 12292
  87.4 399.1 %copy-start.2 = (f32[1024]{0:T(1024)S(1)}, f32[1024]{0:T(1024)}, u32[]{:S(2)}) copy-start(f32[1024]{0:T(1024)} %param.17) | copy-start | bytes 12292
  87.4 703.1 %all-reduce.24.cloned.1.call-start = ((), (), s32[]{:S(2)}) async-start(), calls=%async_computation.3 | async-start | bytes 8388608 | tf_op jit(solution)/shard_map/psum | solution.py:148
  486.5 310.0 %copy-start.3 = (f32[1024]{0:T(1024)S(1)}, f32[1024]{0:T(1024)}, u32[]{:S(2)}) copy-start(f32[1024]{0:T(1024)} %param.16) | copy-start | bytes 12292
  853.3 27.6 %all-to-all-start.1 = ((f32[192,1,128]{2,1,0:T(1,128)}), f32[192,1,128]{2,1,0:T(1,128)S(1)}, u32[]{:S(2)}, u32[]{:S(2)}) async-start(f32[192,1,128]{2,1,0:T(1,128)} %bitcast.21), calls=%async_computation.1 | async-start | bytes 196608 | tf_op jit(solution)/shard_map/all_to_all | solution.py:153
Sparse Core Ops, SparseCore 0:
  87.5 398.7 all-reduce.21
  489.2 301.1 all-reduce.23
